TPU v7x, 32 devices: a whole 2x2x4 slice. The times are simulated.
32 devices in a mesh: parts: 2 (over x), gx: 8 (over z, y), gy: 2 (over core).
Axes of the slice: x: 2, y: 2, z: 4, core: 2. Of those that a mesh axis runs over, the one named last changes fastest.
Arguments:
- field: float32 [2, 4096, 1024], P(None, ('parts', 'gx'), 'gy'), parts along dimension 1, may hold values from -6 to 6
- levels: int32 [4096, 1024], P(('parts', 'gx'), 'gy'), parts along dimension 0, may hold values from 0 to 255
- table: float32 [256], replicated, may hold values from 0 to 3
Outputs:
- near_field: float32 [2, 4096, 1024], P(None, ('parts', 'gx'), 'gy'), parts along dimension 1
- far_field: float32 [2048, 2, 1024], P(('parts', 'gx'), None, 'gy'), parts along dimension 0
There are 2 independent parts, one for each index of `parts`. A program takes and returns all parts, laid end to end along the dimension named above; an argument that names none is the same for every part. Nothing has to cross between parts.
All inputs are finite; a program needn't handle non-finite values.
Results may differ from a plain program's by a relative error of at most 0.0003.
Values sent between devices are 32-bit elements; how exact they have to be, the bound alone decides.
A program may use at most 384 MiB of HBM per device.

v0:
```python
import functools
import math

import jax
import jax.numpy as jnp
from jax import lax
from jax.experimental import pallas as pl
from jax.experimental.pallas import tpu as pltpu
from jax.sharding import PartitionSpec as P

P_SIZE = 1024
Q = 1024
STEPS = 8
HALO = 4 * STEPS
LANES = 128
MESH = pl.DeviceIdType.MESH
F32 = jnp.float32
BF16 = jnp.bfloat16


def place(ix, iy):
    return (lax.axis_index("parts"), ix, iy)


def greet(neighbours):
    barrier = pltpu.get_barrier_semaphore()
    for device in neighbours:
        pl.semaphore_signal(barrier, inc=1, device_id=device, device_id_type=MESH)
    pl.semaphore_wait(barrier, len(neighbours))


def halo_kernel(count_x, field, levels, ext_f, ext_l, send, recv, own):
    rows, cols = levels.shape
    ix = lax.axis_index("gx")
    iy = lax.axis_index("gy")
    above = lax.rem(ix + count_x - 1, count_x)
    below = lax.rem(ix + 1, count_x)
    other = 1 - iy
    moves = (
        (place(ix, other), 0, rows, HALO, True),
        (place(above, iy), 0, HALO, HALO + rows, False),
        (place(below, iy), rows - HALO, HALO, 0, False),
        (place(above, other), 0, HALO, HALO + rows, True),
        (place(below, other), rows - HALO, HALO, 0, True),
    )
    greet([move[0] for move in moves])
    edge = pl.ds(pl.multiple_of((cols - LANES) * other, LANES), LANES)
    copies = []
    for k, (device, start, length, land, side) in enumerate(moves):
        src = pl.ds(start, length)
        dst = pl.ds(land, length)
        src_c = edge if side else pl.ds(0, cols)
        dst_c = pl.ds(cols, LANES) if side else pl.ds(0, cols)
        copies.append(
            pltpu.make_async_remote_copy(
                field.at[:, src, src_c], ext_f.at[:, dst, dst_c], send.at[2 * k], recv.at[2 * k],
                device_id=device, device_id_type=MESH,
            )
        )
        copies.append(
            pltpu.make_async_remote_copy(
                levels.at[src, src_c], ext_l.at[dst, dst_c], send.at[2 * k + 1], recv.at[2 * k + 1],
                device_id=device, device_id_type=MESH,
            )
        )
    for copy in copies:
        copy.start()
    inner = pl.ds(HALO, rows)
    mine = [
        pltpu.make_async_copy(field, ext_f.at[:, inner, pl.ds(0, cols)], own.at[0]),
        pltpu.make_async_copy(levels, ext_l.at[inner, pl.ds(0, cols)], own.at[1]),
    ]
    for copy in mine:
        copy.start()
    for copy in mine:
        copy.wait()
    for copy in copies:
        copy.wait()


def gather_halo(field, levels):
    _, rows, cols = field.shape
    tall, wide = (rows + 2 * HALO, cols + LANES)
    any_space = pl.BlockSpec(memory_space=pl.ANY)
    return pl.pallas_call(
        functools.partial(halo_kernel, lax.axis_size("gx")),
        out_shape=(
            jax.ShapeDtypeStruct((2, tall, wide), F32),
            jax.ShapeDtypeStruct((tall, wide), jnp.int32),
        ),
        in_specs=[any_space] * 2,
        out_specs=(any_space, any_space),
        scratch_shapes=[
            pltpu.SemaphoreType.DMA((10,)),
            pltpu.SemaphoreType.DMA((10,)),
            pltpu.SemaphoreType.DMA((2,)),
        ],
        compiler_params=pltpu.CompilerParams(collective_id=0, has_side_effects=True),
        name="halo",
    )(field, levels)


def heun_kernel(count_x, ext_f, ext_l, table, out, buf_f, buf_l, u, mid, con, weight, sem):
    blocks, tall, _ = buf_l.shape
    deep = tall // 8
    cols = (blocks - 1) * LANES
    rows = tall - 2 * HALO
    ix = lax.axis_index("gx")
    iy = lax.axis_index("gy")
    loads = []
    for j in range(blocks):
        lanes = pl.ds(j * LANES, LANES)
        loads.append(pltpu.make_async_copy(ext_l.at[:, lanes], buf_l.at[j], sem.at[0, j]))
        loads.append(pltpu.make_async_copy(ext_f.at[0, :, lanes], buf_f.at[0, j], sem.at[1, j]))
        loads.append(pltpu.make_async_copy(ext_f.at[1, :, lanes], buf_f.at[1, j], sem.at[2, j]))
    for copy in loads:
        copy.start()
    low = jnp.broadcast_to(table[0:1, :], (8, LANES))
    high = jnp.broadcast_to(table[1:2, :], (8, LANES))
    sub = lax.broadcasted_iota(jnp.int32, (8, LANES), 0)
    lane = lax.broadcasted_iota(jnp.int32, (8, LANES), 1)
    side = jnp.where((lane < LANES // 2) == (iy == 0), 1.0, 0.0).astype(F32)
    top = jnp.where(ix == 0, HALO, 0)
    bottom = jnp.where(ix == count_x - 1, HALO + rows, tall)
    for copy in loads:
        copy.wait()

    def prepare(r, carry):
        row = sub * deep + r
        inside = jnp.where((row >= top) & (row < bottom), 1.0, 0.0).astype(F32)
        for j in range(blocks):
            mask = inside * side if j == blocks - 1 else inside
            lanes = pl.ds(j * LANES, LANES)
            weight[r, :, lanes] = mask * (0.075 / 12.0)
            level = buf_l[j, pl.ds(r, 8, stride=deep), :]
            within = level & (LANES - 1)
            value = jnp.where(
                level < LANES,
                jnp.take_along_axis(low, within, axis=1),
                jnp.take_along_axis(high, within, axis=1),
            )
            con[r, :, lanes] = 12.0 * (value - 5.0)
            for c in range(2):
                u[c, r + 2, :, lanes] = mask * buf_f[c, j, pl.ds(r, 8, stride=deep), :]
        return carry

    lax.fori_loop(0, deep, prepare, 0)

    def wrap(ref):
        for c in range(2):
            for k in range(2):
                ref[c, k] = pltpu.roll(ref[c, deep + k], 1, 0)
                ref[c, deep + 2 + k] = pltpu.roll(ref[c, 2 + k], 7, 0)

    wide = blocks * LANES

    def twelve(ref, c, r):
        v = ref[c, r + 2]
        near = pltpu.roll(v, 1, 1) + pltpu.roll(v, wide - 1, 1) + (ref[c, r + 1] + ref[c, r + 3])
        far = pltpu.roll(v, 2, 1) + pltpu.roll(v, wide - 2, 1) + (ref[c, r] + ref[c, r + 4])
        return 16.0 * near - far + con[r] * v

    def step(_, carry):
        wrap(u)

        @pl.loop(0, deep, unroll=2)
        def _(r):
            w = weight[r]
            mid[0, r + 2] = u[0, r + 2] - w * twelve(u, 1, r)
            mid[1, r + 2] = u[1, r + 2] + w * twelve(u, 0, r)

        wrap(mid)

        @pl.loop(0, deep, unroll=2)
        def _(r):
            w = weight[r]
            u[0, r + 2] = 0.5 * ((u[0, r + 2] + mid[0, r + 2]) - w * twelve(mid, 1, r))
            u[1, r + 2] = 0.5 * ((u[1, r + 2] + mid[1, r + 2]) + w * twelve(mid, 0, r))

        return carry

    lax.fori_loop(0, STEPS, step, 0)

    def unpack(r, carry):
        for j in range(blocks - 1):
            for c in range(2):
                buf_f[c, j, pl.ds(r, 8, stride=deep), :] = u[c, r + 2, :, pl.ds(j * LANES, LANES)]
        return carry

    lax.fori_loop(0, deep, unpack, 0)
    for j in range(blocks - 1):
        for c in range(2):
            out[c, :, pl.ds(j * LANES, LANES)] = buf_f[c, j, pl.ds(HALO, rows), :]


def propagate(ext_f, ext_l, table):
    _, tall, wide = ext_f.shape
    blocks = wide // LANES
    deep = tall // 8
    any_space = pl.BlockSpec(memory_space=pl.ANY)
    vmem = pl.BlockSpec(memory_space=pltpu.VMEM)
    return pl.pallas_call(
        functools.partial(heun_kernel, lax.axis_size("gx")),
        out_shape=jax.ShapeDtypeStruct((2, tall - 2 * HALO, wide - LANES), F32),
        in_specs=[any_space, any_space, vmem],
        out_specs=vmem,
        scratch_shapes=[
            pltpu.VMEM((2, blocks, tall, LANES), F32),
            pltpu.VMEM((blocks, tall, LANES), jnp.int32),
            pltpu.VMEM((2, deep + 4, 8, wide), F32),
            pltpu.VMEM((2, deep + 4, 8, wide), F32),
            pltpu.VMEM((deep, 8, wide), F32),
            pltpu.VMEM((deep, 8, wide), F32),
            pltpu.SemaphoreType.DMA((3, blocks)),
        ],
        compiler_params=pltpu.CompilerParams(vmem_limit_bytes=40 * 1024 * 1024),
        name="heun",
    )(ext_f, ext_l, table.reshape(2, LANES))


def split(x):
    big = x.astype(BF16)
    return (big, (x - big.astype(F32)).astype(BF16))


def dot3(a, b):
    dot = functools.partial(jnp.dot, preferred_element_type=F32)
    return dot(a[0], b[0]) + (dot(a[0], b[1]) + dot(a[1], b[0]))


def far_kernel(
    near, e1c, e1s, e2c, e2s, yac, yas, ybc, ybs, out,
    raw, xc, xs, rhs, yc, ys, acc, from_up, from_dn, band, give, take,
    raw_send, raw_recv, up_send, up_recv, dn_send, dn_recv, side_send, side_recv,
):
    chunks, _, rows, _ = raw.shape
    groups = acc.shape[1]
    p_rows = acc.shape[2]
    half_q = yc.shape[3]
    ix = lax.axis_index("gx")
    iy = lax.axis_index("gy")
    z = ix // 2
    odd = lax.rem(ix, 2)
    count_x = 2 * groups
    pair = place(ix + 1 - 2 * odd, iy)
    higher = place(lax.rem(ix + 2, count_x), iy)
    lower = place(lax.rem(ix + count_x - 2, count_x), iy)
    side = place(ix, 1 - iy)
    greet([pair, higher, lower, side])

    def remote(src, dst, s, r, device):
        return pltpu.make_async_remote_copy(src, dst, s, r, device_id=device, device_id_type=MESH)

    raws = [
        remote(near.at[:, :, pl.ds(c * LANES, LANES)], raw.at[c], raw_send.at[c], raw_recv.at[c], pair)
        for c in range(chunks)
    ]
    for copy in raws:
        copy.start()

    for o in range(groups):
        a_c, a_s = (e1c[o : o + 1, :], e1s[o : o + 1, :])
        for k, part in enumerate(split(a_c * e2c[...] - a_s * e2s[...])):
            xc[k, pl.ds(o * p_rows, p_rows), :] = part
        for k, part in enumerate(split(a_s * e2c[...] + a_c * e2s[...])):
            xs[k, pl.ds(o * p_rows, p_rows), :] = part
    fine = ybc.shape[0]
    for h in range(2):
        q = pl.ds(h * half_q, half_q)
        for o in range(yac.shape[0]):
            a_c, a_s = (yac[o : o + 1, q], yas[o : o + 1, q])
            y = pl.ds(o * fine, fine)
            for k, part in enumerate(split(a_c * ybc[:, q] - a_s * ybs[:, q])):
                yc[h, k, y, :] = part
            for k, part in enumerate(split(a_s * ybc[:, q] + a_c * ybs[:, q])):
                ys[h, k, y, :] = part

    def up_copy(c, o):
        return remote(acc.at[c, o], from_up.at[c, o], up_send.at[c, o], up_recv.at[c, o], higher)

    def dn_copy(c, o):
        return remote(acc.at[c, o], from_dn.at[c, o], dn_send.at[c, o], dn_recv.at[c, o], lower)

    for c in range(chunks):
        raws[c].wait_recv()
        mine = pl.ds(pl.multiple_of(odd * rows, rows), rows)
        theirs = pl.ds(pl.multiple_of((1 - odd) * rows, rows), rows)
        for d in range(2):
            lanes = pl.ds(d * LANES, LANES)
            for k, part in enumerate(split(near[d, :, pl.ds(c * LANES, LANES)])):
                rhs[k, mine, lanes] = part
            for k, part in enumerate(split(raw[c, d])):
                rhs[k, theirs, lanes] = part
        right = (rhs[0], rhs[1])
        by_cos = dot3((xc[0], xc[1]), right)
        by_sin = dot3((xs[0], xs[1]), right)
        re = by_cos[:, :LANES] + by_sin[:, LANES:]
        im = by_cos[:, LANES:] - by_sin[:, :LANES]
        for o in range(groups):
            acc[c, o, :, pl.ds(0, LANES)] = re[o * p_rows : (o + 1) * p_rows]
            acc[c, o, :, pl.ds(LANES, LANES)] = im[o * p_rows : (o + 1) * p_rows]
        for k in range(groups):
            far_up, far_dn = (groups - 1 - k, k)

            @pl.when(z < far_up)
            def _():
                @pl.when(z > 0)
                def _():
                    up_copy(c, far_up).wait_recv()
                    acc[c, far_up] += from_up[c, far_up]

                up_copy(c, far_up).start()

            @pl.when(z > far_dn)
            def _():
                @pl.when(z < groups - 1)
                def _():
                    dn_copy(c, far_dn).wait_recv()
                    acc[c, far_dn] += from_dn[c, far_dn]

                dn_copy(c, far_dn).start()

    for c in range(chunks):
        for o in range(groups):

            @pl.when(z == o)
            def _():
                if o > 0:
                    up_copy(c, o).wait_recv()
                if o < groups - 1:
                    dn_copy(c, o).wait_recv()
                total = acc[c, o]
                if o > 0:
                    total = total + from_up[c, o]
                if o < groups - 1:
                    total = total + from_dn[c, o]
                for k, part in enumerate(split(total)):
                    band[k, pl.ds(0, p_rows), pl.ds(c * LANES, LANES)] = part[:, :LANES]
                    band[k, pl.ds(p_rows, p_rows), pl.ds(c * LANES, LANES)] = part[:, LANES:]

    left = (band[0], band[1])

    def angles(h):
        by_cos = dot3(left, (yc[h, 0], yc[h, 1]))
        by_sin = dot3(left, (ys[h, 0], ys[h, 1]))
        return (by_cos[:p_rows] + by_sin[p_rows:], by_cos[p_rows:] - by_sin[:p_rows])

    re, im = angles(1 - iy)
    give[0] = re
    give[1] = im
    swap = remote(give, take, side_send.at[0], side_recv.at[0], side)
    swap.start()
    re, im = angles(iy)
    swap.wait_recv()
    out[0] = re + take[0]
    out[1] = im + take[1]

    swap.wait_send()
    for copy in raws:
        copy.wait_send()
    for c in range(chunks):
        for o in range(groups):

            @pl.when(z < o)
            def _():
                up_copy(c, o).wait_send()

            @pl.when(z > o)
            def _():
                dn_copy(c, o).wait_send()


def turn(phase, total, scale):
    angle = 2.0 * math.pi / total * (phase % total).astype(F32)
    return (jnp.cos(angle) * scale, jnp.sin(angle) * scale)


def tables(rows, cols, count_x, count_y):
    index_x = lax.axis_index("gx")
    index_y = lax.axis_index("gy")
    total_x = rows * count_x
    total_y = cols * count_y
    p_rows = P_SIZE // count_x
    x = (index_x // 2) * 2 * rows + jnp.arange(2 * rows, dtype=jnp.int32)
    first = (2 * jnp.arange(count_x // 2, dtype=jnp.int32) + index_x % 2) * p_rows
    base = first + total_x - P_SIZE // 2
    e1 = turn(base[:, None] * x[None, :], total_x, 1.0 / math.sqrt(total_x))
    e2 = turn(jnp.arange(p_rows, dtype=jnp.int32)[:, None] * x[None, :], total_x, 1.0)
    fine = 32
    q = jnp.arange(Q, dtype=jnp.int32) + total_y - Q // 2
    coarse = index_y * cols + fine * jnp.arange(cols // fine, dtype=jnp.int32)
    ya = turn(coarse[:, None] * q[None, :], total_y, 1.0 / math.sqrt(total_y))
    yb = turn(jnp.arange(fine, dtype=jnp.int32)[:, None] * q[None, :], total_y, 1.0)
    return (*e1, *e2, *ya, *yb)


def far(near, angles, count_x):
    _, rows, cols = near.shape
    groups = count_x // 2
    p_rows = P_SIZE // count_x
    chunks = cols // LANES
    half_q = Q // 2
    vmem = pl.BlockSpec(memory_space=pltpu.VMEM)
    dma = pltpu.SemaphoreType.DMA
    stage = pltpu.VMEM((chunks, groups, p_rows, 2 * LANES), F32)
    return pl.pallas_call(
        far_kernel,
        out_shape=jax.ShapeDtypeStruct((2, p_rows, half_q), F32),
        in_specs=[vmem] * 9,
        out_specs=vmem,
        scratch_shapes=[
            pltpu.VMEM((chunks, 2, rows, LANES), F32),
            pltpu.VMEM((2, groups * p_rows, 2 * rows), BF16),
            pltpu.VMEM((2, groups * p_rows, 2 * rows), BF16),
            pltpu.VMEM((2, 2 * rows, 2 * LANES), BF16),
            pltpu.VMEM((2, 2, cols, half_q), BF16),
            pltpu.VMEM((2, 2, cols, half_q), BF16),
            stage,
            stage,
            stage,
            pltpu.VMEM((2, 2 * p_rows, cols), BF16),
            pltpu.VMEM((2, p_rows, half_q), F32),
            pltpu.VMEM((2, p_rows, half_q), F32),
            dma((chunks,)),
            dma((chunks,)),
            dma((chunks, groups)),
            dma((chunks, groups)),
            dma((chunks, groups)),
            dma((chunks, groups)),
            dma((1,)),
            dma((1,)),
        ],
        compiler_params=pltpu.CompilerParams(
            collective_id=1, has_side_effects=True, vmem_limit_bytes=48 * 1024 * 1024
        ),
        name="far",
    )(near, *angles)


def on_device(field, levels, table):
    _, rows, cols = field.shape
    count_x = lax.axis_size("gx")
    angles = tables(rows, cols, count_x, lax.axis_size("gy"))
    ext_f, ext_l = gather_halo(field, levels)
    near = propagate(ext_f, ext_l, table)
    return (near, jnp.transpose(far(near, angles, count_x), (1, 0, 2)))


def solution(mesh):
    in_specs = (P(None, ("parts", "gx"), "gy"), P(("parts", "gx"), "gy"), P())
    out_specs = (P(None, ("parts", "gx"), "gy"), P(("parts", "gx"), None, "gy"))
    return jax.shard_map(
        on_device, mesh=mesh, in_specs=in_specs, out_specs=out_specs, check_vma=False
    )
```

profile of v0, /device:TPU:0, one launch (start us, length us, event | category | flops | bytes accessed | tf_op | source)
XLA Modules:
  0.0 180.8 jit_solution(1732908912943181535)
XLA Ops:
  0.6 55.0 %halo.1 = (f32[2,320,640]{2,1,0:T(8,128)}, s32[320,640]{1,0:T(8,128)}) custom-call(f32[2,256,512]{2,1,0:T(8,128)} %field.1, s32[256,512]{1,0:T(8,128)} %levels.1), custom_call_target="tpu_custom_call" | custom-call | tf_op jit(solution)/shard_map/halo/pallas_call | solution.py:85
  55.7 0.0 copy-start.1
  55.7 1.4 copy-done.1
  57.1 0.0 copy-start.2
  57.1 1.1 copy-done.2
  58.3 0.0 copy-start.3
  58.3 0.7 copy-done.3
  58.9 57.0 %heun.1.near = f32[2,256,512]{2,1,0:T(8,128)} custom-call(f32[2,320,640]{2,1,0:T(8,128)S(1)} %copy-done.1, s32[320,640]{1,0:T(8,128)S(1)} %copy-done.2, f32[2,128]{1,0:T(2,128)S(1)} %bitcast.3), custom_call_target="tpu_custom_call" | custom-call | tf_op jit(solution)/shard_map/heun/pallas_call | solution.py:202
  116.0 0.2 sine_multiply_fusion.1
  116.1 1.0 fusion.11
  117.2 0.3 sine_multiply_fusion
  117.5 0.5 fusion.17
  118.1 0.0 copy-start
  118.1 1.2 copy-done
  119.3 60.3 %far.1 = f32[2,128,512]{2,1,0:T(8,128)S(1)} custom-call(f32[2,256,512]{2,1,0:T(8,128)S(1)} %copy-done, f32[4,512]{1,0:T(4,128)S(1)} %get-tuple-element.13.e1c, f32[4,512]{1,0:T(4,128)S(1)} %get-tuple-element.12.e1s, f32[128,512]{1,0:T(8,128)S(1)} %get-tuple-element.15.e2c, f32[128,512]{1,0:T(8,128)S(1)} %get-tuple-element.14.e2s, ...), custom_call_target="tpu_custom_call" | custom-call | tf_op jit(solution)/shard_map/far/pallas_call | solution.py:406
  179.6 1.2 copy.5
  (4 shorter events, 0.0 us)
Async XLA Ops:
  55.7 1.4 copy-start.1
  57.1 1.1 copy-start.2
  58.3 0.7 copy-start.3
  118.1 1.2 copy-start
where the time goes:
time: 181 us
  Pallas kernels  172 us (95%)
  local copies, waits for them, and re-layouts  5.67 us (3%)
  other arithmetic  2.08 us (1%)
    pallas_call x1, Pallas kernels, far(): pl.pallas_call(far_kernel, out_shape=jax.ShapeDtypeStruct((2, p_rows, hal...  60.3 us
    pallas_call x1, Pallas kernels, propagate(): pl.pallas_call(functools.partial(heun_kernel, lax.axis_size('gx')), out_s...  57 us
    pallas_call x1, Pallas kernels, gather_halo(): pl.pallas_call(functools.partial(halo_kernel, lax.axis_size('gx')), out_s...  55 us
    unnamed x9, local copies, waits for them, and re-layouts  5.67 us

commit v1 on v0

--- a/solution.py
+++ b/solution.py
@@ -29,7 +29,7 @@
     pl.semaphore_wait(barrier, len(neighbours))
 
 
-def halo_kernel(count_x, field, levels, ext_f, ext_l, send, recv, own):
+def halo_kernel(count_x, field, levels, ext_f, ext_l, send, recv):
     rows, cols = levels.shape
     ix = lax.axis_index("gx")
     iy = lax.axis_index("gy")
@@ -66,14 +66,8 @@
     for copy in copies:
         copy.start()
     inner = pl.ds(HALO, rows)
-    mine = [
-        pltpu.make_async_copy(field, ext_f.at[:, inner, pl.ds(0, cols)], own.at[0]),
-        pltpu.make_async_copy(levels, ext_l.at[inner, pl.ds(0, cols)], own.at[1]),
-    ]
-    for copy in mine:
-        copy.start()
-    for copy in mine:
-        copy.wait()
+    ext_f[:, inner, pl.ds(0, cols)] = field[...]
+    ext_l[inner, pl.ds(0, cols)] = levels[...]
     for copy in copies:
         copy.wait()
 
@@ -81,57 +75,72 @@
 def gather_halo(field, levels):
     _, rows, cols = field.shape
     tall, wide = (rows + 2 * HALO, cols + LANES)
-    any_space = pl.BlockSpec(memory_space=pl.ANY)
+    vmem = pl.BlockSpec(memory_space=pltpu.VMEM)
     return pl.pallas_call(
         functools.partial(halo_kernel, lax.axis_size("gx")),
         out_shape=(
             jax.ShapeDtypeStruct((2, tall, wide), F32),
             jax.ShapeDtypeStruct((tall, wide), jnp.int32),
         ),
-        in_specs=[any_space] * 2,
-        out_specs=(any_space, any_space),
+        in_specs=[vmem] * 2,
+        out_specs=(vmem, vmem),
         scratch_shapes=[
             pltpu.SemaphoreType.DMA((10,)),
             pltpu.SemaphoreType.DMA((10,)),
-            pltpu.SemaphoreType.DMA((2,)),
         ],
         compiler_params=pltpu.CompilerParams(collective_id=0, has_side_effects=True),
         name="halo",
     )(field, levels)
 
 
-def heun_kernel(count_x, ext_f, ext_l, table, out, buf_f, buf_l, u, mid, con, weight, sem):
+def shuffle(x, order):
+    parts = [x.astype(BF16)]
+    for _ in range(2):
+        x = x - parts[-1].astype(F32)
+        parts.append(x.astype(BF16))
+    return sum(jnp.dot(part, order, preferred_element_type=F32) for part in parts)
+
+
+def spread_order(shape, blocks, dim):
+    spread = lax.broadcasted_iota(jnp.int32, shape, dim)
+    plain = lax.broadcasted_iota(jnp.int32, shape, 1 - dim)
+    return jnp.where(plain == (spread & (LANES - 1)) * blocks + spread // LANES, 1.0, 0.0).astype(BF16)
+
+
+def heun_kernel(count_x, ext_f, ext_l, table, out, buf_f, buf_l, u, mid, con, weight):
     blocks, tall, _ = buf_l.shape
     deep = tall // 8
-    cols = (blocks - 1) * LANES
+    wide = blocks * LANES
+    cols = wide - LANES
     rows = tall - 2 * HALO
     ix = lax.axis_index("gx")
     iy = lax.axis_index("gy")
-    loads = []
+    order = spread_order((wide, wide), blocks, 1)
+    for c in range(2):
+        spread = shuffle(ext_f[c], order)
+        for j in range(blocks):
+            buf_f[c, j] = spread[:, j * LANES : (j + 1) * LANES]
+    spread = jnp.dot(ext_l[...].astype(F32).astype(BF16), order, preferred_element_type=F32)
     for j in range(blocks):
-        lanes = pl.ds(j * LANES, LANES)
-        loads.append(pltpu.make_async_copy(ext_l.at[:, lanes], buf_l.at[j], sem.at[0, j]))
-        loads.append(pltpu.make_async_copy(ext_f.at[0, :, lanes], buf_f.at[0, j], sem.at[1, j]))
-        loads.append(pltpu.make_async_copy(ext_f.at[1, :, lanes], buf_f.at[1, j], sem.at[2, j]))
-    for copy in loads:
-        copy.start()
+        buf_l[j] = spread[:, j * LANES : (j + 1) * LANES].astype(jnp.int32)
     low = jnp.broadcast_to(table[0:1, :], (8, LANES))
     high = jnp.broadcast_to(table[1:2, :], (8, LANES))
     sub = lax.broadcasted_iota(jnp.int32, (8, LANES), 0)
     lane = lax.broadcasted_iota(jnp.int32, (8, LANES), 1)
-    side = jnp.where((lane < LANES // 2) == (iy == 0), 1.0, 0.0).astype(F32)
     top = jnp.where(ix == 0, HALO, 0)
     bottom = jnp.where(ix == count_x - 1, HALO + rows, tall)
-    for copy in loads:
-        copy.wait()
+    middle = cols + LANES // 2
+    sides = []
+    for j in range(blocks):
+        col = lane * blocks + j
+        sides.append(jnp.where((col < cols) | ((col < middle) == (iy == 0)), 1.0, 0.0).astype(F32))
 
     def prepare(r, carry):
         row = sub * deep + r
         inside = jnp.where((row >= top) & (row < bottom), 1.0, 0.0).astype(F32)
         for j in range(blocks):
-            mask = inside * side if j == blocks - 1 else inside
-            lanes = pl.ds(j * LANES, LANES)
-            weight[r, :, lanes] = mask * (0.075 / 12.0)
+            mask = inside * sides[j]
+            weight[j, r] = mask * (0.075 / 12.0)
             level = buf_l[j, pl.ds(r, 8, stride=deep), :]
             within = level & (LANES - 1)
             value = jnp.where(
@@ -139,79 +148,91 @@
                 jnp.take_along_axis(low, within, axis=1),
                 jnp.take_along_axis(high, within, axis=1),
             )
-            con[r, :, lanes] = 12.0 * (value - 5.0)
+            con[j, r] = 12.0 * (value - 5.0)
             for c in range(2):
-                u[c, r + 2, :, lanes] = mask * buf_f[c, j, pl.ds(r, 8, stride=deep), :]
+                u[c, j, r + 2] = mask * buf_f[c, j, pl.ds(r, 8, stride=deep), :]
         return carry
 
     lax.fori_loop(0, deep, prepare, 0)
 
     def wrap(ref):
         for c in range(2):
-            for k in range(2):
-                ref[c, k] = pltpu.roll(ref[c, deep + k], 1, 0)
-                ref[c, deep + 2 + k] = pltpu.roll(ref[c, 2 + k], 7, 0)
-
-    wide = blocks * LANES
+            for j in range(blocks):
+                for k in range(2):
+                    ref[c, j, k] = pltpu.roll(ref[c, j, deep + k], 1, 0)
+                    ref[c, j, deep + 2 + k] = pltpu.roll(ref[c, j, 2 + k], 7, 0)
+
+    tile = 4
 
     def twelve(ref, c, r):
-        v = ref[c, r + 2]
-        near = pltpu.roll(v, 1, 1) + pltpu.roll(v, wide - 1, 1) + (ref[c, r + 1] + ref[c, r + 3])
-        far = pltpu.roll(v, 2, 1) + pltpu.roll(v, wide - 2, 1) + (ref[c, r] + ref[c, r + 4])
-        return 16.0 * near - far + con[r] * v
+        v = [[ref[c, j, r + k] for k in range(tile + 4)] for j in range(blocks)]
+        line = {j: v[j][2 : tile + 2] for j in range(blocks)}
+        for k in range(2):
+            line[k - 2] = [pltpu.roll(x, 1, 1) for x in line[blocks + k - 2]]
+            line[blocks + k] = [pltpu.roll(x, LANES - 1, 1) for x in line[k]]
+        for j in range(blocks):
+            for t in range(tile):
+                near = (line[j - 1][t] + line[j + 1][t]) + (v[j][t + 1] + v[j][t + 3])
+                far = (line[j - 2][t] + line[j + 2][t]) + (v[j][t] + v[j][t + 4])
+                yield j, t, weight[j, r + t] * (16.0 * near - far + con[j, r + t] * v[j][t + 2])
 
     def step(_, carry):
         wrap(u)
 
-        @pl.loop(0, deep, unroll=2)
-        def _(r):
-            w = weight[r]
-            mid[0, r + 2] = u[0, r + 2] - w * twelve(u, 1, r)
-            mid[1, r + 2] = u[1, r + 2] + w * twelve(u, 0, r)
+        @pl.loop(0, deep // tile)
+        def _(block):
+            r = block * tile
+            for j, t, k1 in twelve(u, 1, r):
+                mid[0, j, r + t + 2] = u[0, j, r + t + 2] - k1
+            for j, t, k1 in twelve(u, 0, r):
+                mid[1, j, r + t + 2] = u[1, j, r + t + 2] + k1
 
         wrap(mid)
 
-        @pl.loop(0, deep, unroll=2)
-        def _(r):
-            w = weight[r]
-            u[0, r + 2] = 0.5 * ((u[0, r + 2] + mid[0, r + 2]) - w * twelve(mid, 1, r))
-            u[1, r + 2] = 0.5 * ((u[1, r + 2] + mid[1, r + 2]) + w * twelve(mid, 0, r))
+        @pl.loop(0, deep // tile)
+        def _(block):
+            r = block * tile
+            for j, t, k2 in twelve(mid, 1, r):
+                u[0, j, r + t + 2] = 0.5 * ((u[0, j, r + t + 2] + mid[0, j, r + t + 2]) - k2)
+            for j, t, k2 in twelve(mid, 0, r):
+                u[1, j, r + t + 2] = 0.5 * ((u[1, j, r + t + 2] + mid[1, j, r + t + 2]) + k2)
 
         return carry
 
     lax.fori_loop(0, STEPS, step, 0)
 
     def unpack(r, carry):
-        for j in range(blocks - 1):
+        for j in range(blocks):
             for c in range(2):
-                buf_f[c, j, pl.ds(r, 8, stride=deep), :] = u[c, r + 2, :, pl.ds(j * LANES, LANES)]
+                buf_f[c, j, pl.ds(r, 8, stride=deep), :] = u[c, j, r + 2]
         return carry
 
     lax.fori_loop(0, deep, unpack, 0)
-    for j in range(blocks - 1):
-        for c in range(2):
-            out[c, :, pl.ds(j * LANES, LANES)] = buf_f[c, j, pl.ds(HALO, rows), :]
+    order = spread_order((wide, cols), blocks, 0)
+    for c in range(2):
+        spread = jnp.concatenate([buf_f[c, j, pl.ds(HALO, rows), :] for j in range(blocks)], axis=1)
+        out[c] = shuffle(spread, order)
 
 
 def propagate(ext_f, ext_l, table):
     _, tall, wide = ext_f.shape
     blocks = wide // LANES
     deep = tall // 8
-    any_space = pl.BlockSpec(memory_space=pl.ANY)
     vmem = pl.BlockSpec(memory_space=pltpu.VMEM)
+    state = pltpu.VMEM((2, blocks, deep + 4, 8, LANES), F32)
+    factor = pltpu.VMEM((blocks, deep, 8, LANES), F32)
     return pl.pallas_call(
         functools.partial(heun_kernel, lax.axis_size("gx")),
         out_shape=jax.ShapeDtypeStruct((2, tall - 2 * HALO, wide - LANES), F32),
-        in_specs=[any_space, any_space, vmem],
+        in_specs=[vmem, vmem, vmem],
         out_specs=vmem,
         scratch_shapes=[
             pltpu.VMEM((2, blocks, tall, LANES), F32),
             pltpu.VMEM((blocks, tall, LANES), jnp.int32),
-            pltpu.VMEM((2, deep + 4, 8, wide), F32),
-            pltpu.VMEM((2, deep + 4, 8, wide), F32),
-            pltpu.VMEM((deep, 8, wide), F32),
-            pltpu.VMEM((deep, 8, wide), F32),
-            pltpu.SemaphoreType.DMA((3, blocks)),
+            state,
+            state,
+            factor,
+            factor,
         ],
         compiler_params=pltpu.CompilerParams(vmem_limit_bytes=40 * 1024 * 1024),
         name="heun",

time: 181 us -> 117 us (0.65)
  Pallas kernels: 172 us -> 109 us
    pallas_call x1, Pallas kernels: 55 us -> 18.6 us  [gather_halo(): pl.pallas_call(functools.partial(halo_kernel, lax.axis_size('gx')), out_s...]
    pallas_call x1, Pallas kernels: 57 us -> 27.6 us  [propagate(): pl.pallas_call(functools.partial(heun_kernel, lax.axis_size('gx')), out_s...]
    pallas_call x1, Pallas kernels: 60.3 us -> 62.4 us  [far(): pl.pallas_call(far_kernel, out_shape=jax.ShapeDtypeStruct((2, p_rows, hal...]
where the time goes in v1:
time: 117 us
  Pallas kernels  109 us (93%)
  local copies, waits for them, and re-layouts  5.67 us (5%)
  other arithmetic  2.08 us (2%)
    pallas_call x1, Pallas kernels, far(): pl.pallas_call(far_kernel, out_shape=jax.ShapeDtypeStruct((2, p_rows, hal...  62.4 us
    pallas_call x1, Pallas kernels, propagate(): pl.pallas_call(functools.partial(heun_kernel, lax.axis_size('gx')), out_s...  27.6 us
    pallas_call x1, Pallas kernels, gather_halo(): pl.pallas_call(functools.partial(halo_kernel, lax.axis_size('gx')), out_s...  18.6 us
    unnamed x9, local copies, waits for them, and re-layouts  5.67 us

profile of v1, /device:TPU:0, one launch (start us, length us, event | category | flops | bytes accessed | tf_op | source)
XLA Modules:
  0.0 116.9 jit_solution(1588053957784647073)
XLA Ops:
  0.6 18.6 %halo.1 = (f32[2,320,640]{2,1,0:T(8,128)}, s32[320,640]{1,0:T(8,128)}) custom-call(f32[2,256,512]{2,1,0:T(8,128)} %field.1, s32[256,512]{1,0:T(8,128)} %levels.1), custom_call_target="tpu_custom_call" | custom-call | tf_op jit(solution)/shard_map/halo/pallas_call | solution.py:79
  19.2 0.0 copy-start.1
  19.2 1.4 %copy-done.1 = f32[2,320,640]{2,1,0:T(8,128)S(1)} copy-done((f32[2,320,640]{2,1,0:T(8,128)S(1)}, f32[2,320,640]{2,1,0:T(8,128)}, u32[]{:S(2)}) %copy-start.1) | copy-done | bytes 1638424
  20.6 0.0 copy-start.2
  20.6 1.1 copy-done.2
  21.8 0.0 copy-start.3
  21.8 0.7 copy-done.3
  22.5 27.6 %heun.1.near = f32[2,256,512]{2,1,0:T(8,128)} custom-call(f32[2,320,640]{2,1,0:T(8,128)S(1)} %copy-done.1, s32[320,640]{1,0:T(8,128)S(1)} %copy-done.2, f32[2,128]{1,0:T(2,128)S(1)} %bitcast.3), custom_call_target="tpu_custom_call" | custom-call | tf_op jit(solution)/shard_map/heun/pallas_call | solution.py:224
  50.0 0.2 sine_multiply_fusion.1
  50.2 1.0 fusion.11
  51.2 0.3 sine_multiply_fusion
  51.6 0.5 fusion.17
  52.1 0.0 copy-start
  52.1 1.2 %copy-done = f32[2,256,512]{2,1,0:T(8,128)S(1)} copy-done((f32[2,256,512]{2,1,0:T(8,128)S(1)}, f32[2,256,512]{2,1,0:T(8,128)}, u32[]{:S(2)}) %copy-start) | copy-done | bytes 1048600
  53.4 62.4 %far.1 = f32[2,128,512]{2,1,0:T(8,128)S(1)} custom-call(f32[2,256,512]{2,1,0:T(8,128)S(1)} %copy-done, f32[4,512]{1,0:T(4,128)S(1)} %get-tuple-element.13.e1c, f32[4,512]{1,0:T(4,128)S(1)} %get-tuple-element.12.e1s, f32[128,512]{1,0:T(8,128)S(1)} %get-tuple-element.15.e2c, f32[128,512]{1,0:T(8,128)S(1)} %get-tuple-element.14.e2s, ...), custom_call_target="tpu_custom_call" | custom-call | tf_op jit(solution)/shard_map/far/pallas_call | solution.py:427
  115.8 1.2 %copy.5 = f32[128,2,512]{2,1,0:T(2,128)} copy(f32[128,2,512]{2,0,1:T(8,128)S(1)} %bitcast.2) | data formatting | bytes 1048576
  (4 shorter events, 0.0 us)
Async XLA Ops:
  19.2 1.4 %copy-start.1 = (f32[2,320,640]{2,1,0:T(8,128)S(1)}, f32[2,320,640]{2,1,0:T(8,128)}, u32[]{:S(2)}) copy-start(f32[2,320,640]{2,1,0:T(8,128)} %get-tuple-element.4.ext_f) | copy-start | bytes 4915204
  20.6 1.1 copy-start.2
  21.8 0.7 copy-start.3
  52.1 1.2 %copy-start = (f32[2,256,512]{2,1,0:T(8,128)S(1)}, f32[2,256,512]{2,1,0:T(8,128)}, u32[]{:S(2)}) copy-start(f32[2,256,512]{2,1,0:T(8,128)} %heun.1.near) | copy-start | bytes 3145732

commit v2 on v1

--- a/solution.py
+++ b/solution.py
@@ -29,65 +29,95 @@
     pl.semaphore_wait(barrier, len(neighbours))
 
 
-def halo_kernel(count_x, field, levels, ext_f, ext_l, send, recv):
+def halo_kernel(count_x, field, levels, rows_f, rows_l, side_f, side_l, send, recv):
     rows, cols = levels.shape
     ix = lax.axis_index("gx")
     iy = lax.axis_index("gy")
     above = lax.rem(ix + count_x - 1, count_x)
     below = lax.rem(ix + 1, count_x)
     other = 1 - iy
-    moves = (
-        (place(ix, other), 0, rows, HALO, True),
-        (place(above, iy), 0, HALO, HALO + rows, False),
-        (place(below, iy), rows - HALO, HALO, 0, False),
-        (place(above, other), 0, HALO, HALO + rows, True),
-        (place(below, other), rows - HALO, HALO, 0, True),
-    )
-    greet([move[0] for move in moves])
+    greet([place(ix, other), place(above, iy), place(below, iy), place(above, other), place(below, other)])
     edge = pl.ds(pl.multiple_of((cols - LANES) * other, LANES), LANES)
-    copies = []
-    for k, (device, start, length, land, side) in enumerate(moves):
-        src = pl.ds(start, length)
-        dst = pl.ds(land, length)
-        src_c = edge if side else pl.ds(0, cols)
-        dst_c = pl.ds(cols, LANES) if side else pl.ds(0, cols)
-        copies.append(
+    all_c = pl.ds(0, cols)
+    out_c = pl.ds(cols, LANES)
+    first = pl.ds(0, HALO)
+    last = pl.ds(rows - HALO, HALO)
+    whole = pl.ds(0, rows)
+
+    def move(k, device, src, src_c, dst_f, dst_l):
+        pairs = ((field.at[:, src, src_c], dst_f), (levels.at[src, src_c], dst_l))
+        return [
             pltpu.make_async_remote_copy(
-                field.at[:, src, src_c], ext_f.at[:, dst, dst_c], send.at[2 * k], recv.at[2 * k],
-                device_id=device, device_id_type=MESH,
+                a, b, send.at[2 * k + i], recv.at[2 * k + i], device_id=device, device_id_type=MESH
             )
-        )
-        copies.append(
-            pltpu.make_async_remote_copy(
-                levels.at[src, src_c], ext_l.at[dst, dst_c], send.at[2 * k + 1], recv.at[2 * k + 1],
-                device_id=device, device_id_type=MESH,
-            )
-        )
-    for copy in copies:
+            for i, (a, b) in enumerate(pairs)
+        ]
+
+    def land(end, lanes):
+        return (rows_f.at[end, :, :, lanes], rows_l.at[end, :, lanes])
+
+    upward = move(1, place(above, iy), first, all_c, *land(1, all_c))
+    upward += move(3, place(above, other), first, edge, *land(1, out_c))
+    downward = move(2, place(below, iy), last, all_c, *land(0, all_c))
+    downward += move(4, place(below, other), last, edge, *land(0, out_c))
+    across = move(0, place(ix, other), whole, edge, side_f, side_l)
+
+    @pl.when(ix > 0)
+    def _():
+        for copy in upward:
+            copy.start()
+
+    @pl.when(ix < count_x - 1)
+    def _():
+        for copy in downward:
+            copy.start()
+
+    for copy in across:
         copy.start()
-    inner = pl.ds(HALO, rows)
-    ext_f[:, inner, pl.ds(0, cols)] = field[...]
-    ext_l[inner, pl.ds(0, cols)] = levels[...]
-    for copy in copies:
+
+    @pl.when(ix == 0)
+    def _():
+        rows_f[0] = jnp.zeros_like(rows_f[0])
+        rows_l[0] = jnp.zeros_like(rows_l[0])
+
+    @pl.when(ix == count_x - 1)
+    def _():
+        rows_f[1] = jnp.zeros_like(rows_f[1])
+        rows_l[1] = jnp.zeros_like(rows_l[1])
+
+    for copy in across:
         copy.wait()
+
+    @pl.when(ix > 0)
+    def _():
+        for copy in downward:
+            copy.wait_recv()
+        for copy in upward:
+            copy.wait_send()
+
+    @pl.when(ix < count_x - 1)
+    def _():
+        for copy in upward:
+            copy.wait_recv()
+        for copy in downward:
+            copy.wait_send()
 
 
 def gather_halo(field, levels):
     _, rows, cols = field.shape
-    tall, wide = (rows + 2 * HALO, cols + LANES)
+    wide = cols + LANES
     vmem = pl.BlockSpec(memory_space=pltpu.VMEM)
     return pl.pallas_call(
         functools.partial(halo_kernel, lax.axis_size("gx")),
         out_shape=(
-            jax.ShapeDtypeStruct((2, tall, wide), F32),
-            jax.ShapeDtypeStruct((tall, wide), jnp.int32),
+            jax.ShapeDtypeStruct((2, 2, HALO, wide), F32),
+            jax.ShapeDtypeStruct((2, HALO, wide), jnp.int32),
+            jax.ShapeDtypeStruct((2, rows, LANES), F32),
+            jax.ShapeDtypeStruct((rows, LANES), jnp.int32),
         ),
         in_specs=[vmem] * 2,
-        out_specs=(vmem, vmem),
-        scratch_shapes=[
-            pltpu.SemaphoreType.DMA((10,)),
-            pltpu.SemaphoreType.DMA((10,)),
-        ],
+        out_specs=(vmem,) * 4,
+        scratch_shapes=[pltpu.SemaphoreType.DMA((10,)), pltpu.SemaphoreType.DMA((10,))],
         compiler_params=pltpu.CompilerParams(collective_id=0, has_side_effects=True),
         name="halo",
     )(field, levels)
@@ -107,7 +137,9 @@
     return jnp.where(plain == (spread & (LANES - 1)) * blocks + spread // LANES, 1.0, 0.0).astype(BF16)
 
 
-def heun_kernel(count_x, ext_f, ext_l, table, out, buf_f, buf_l, u, mid, con, weight):
+def heun_kernel(
+    count_x, field, levels, rows_f, rows_l, side_f, side_l, table, out, buf_f, buf_l, u, mid, con, weight
+):
     blocks, tall, _ = buf_l.shape
     deep = tall // 8
     wide = blocks * LANES
@@ -116,13 +148,18 @@
     ix = lax.axis_index("gx")
     iy = lax.axis_index("gy")
     order = spread_order((wide, wide), blocks, 1)
+    pieces = ((0, HALO), (HALO, rows), (HALO + rows, HALO))
     for c in range(2):
-        spread = shuffle(ext_f[c], order)
+        body = jnp.concatenate([field[c], side_f[c]], axis=1)
+        for (start, length), part in zip(pieces, (rows_f[0, c], body, rows_f[1, c])):
+            spread = shuffle(part, order)
+            for j in range(blocks):
+                buf_f[c, j, pl.ds(start, length), :] = spread[:, j * LANES : (j + 1) * LANES]
+    body = jnp.concatenate([levels[...], side_l[...]], axis=1)
+    for (start, length), part in zip(pieces, (rows_l[0], body, rows_l[1])):
+        spread = jnp.dot(part.astype(F32).astype(BF16), order, preferred_element_type=F32)
         for j in range(blocks):
-            buf_f[c, j] = spread[:, j * LANES : (j + 1) * LANES]
-    spread = jnp.dot(ext_l[...].astype(F32).astype(BF16), order, preferred_element_type=F32)
-    for j in range(blocks):
-        buf_l[j] = spread[:, j * LANES : (j + 1) * LANES].astype(jnp.int32)
+            buf_l[j, pl.ds(start, length), :] = spread[:, j * LANES : (j + 1) * LANES].astype(jnp.int32)
     low = jnp.broadcast_to(table[0:1, :], (8, LANES))
     high = jnp.broadcast_to(table[1:2, :], (8, LANES))
     sub = lax.broadcasted_iota(jnp.int32, (8, LANES), 0)
@@ -214,17 +251,18 @@
         out[c] = shuffle(spread, order)
 
 
-def propagate(ext_f, ext_l, table):
-    _, tall, wide = ext_f.shape
-    blocks = wide // LANES
+def propagate(field, levels, halo, table):
+    _, rows, cols = field.shape
+    tall = rows + 2 * HALO
+    blocks = cols // LANES + 1
     deep = tall // 8
     vmem = pl.BlockSpec(memory_space=pltpu.VMEM)
     state = pltpu.VMEM((2, blocks, deep + 4, 8, LANES), F32)
     factor = pltpu.VMEM((blocks, deep, 8, LANES), F32)
     return pl.pallas_call(
         functools.partial(heun_kernel, lax.axis_size("gx")),
-        out_shape=jax.ShapeDtypeStruct((2, tall - 2 * HALO, wide - LANES), F32),
-        in_specs=[vmem, vmem, vmem],
+        out_shape=jax.ShapeDtypeStruct((2, rows, cols), F32),
+        in_specs=[vmem] * 7,
         out_specs=vmem,
         scratch_shapes=[
             pltpu.VMEM((2, blocks, tall, LANES), F32),
@@ -236,7 +274,7 @@
         ],
         compiler_params=pltpu.CompilerParams(vmem_limit_bytes=40 * 1024 * 1024),
         name="heun",
-    )(ext_f, ext_l, table.reshape(2, LANES))
+    )(field, levels, *halo, table.reshape(2, LANES))
 
 
 def split(x):
@@ -251,7 +289,7 @@
 
 def far_kernel(
     near, e1c, e1s, e2c, e2s, yac, yas, ybc, ybs, out,
-    raw, xc, xs, rhs, yc, ys, acc, from_up, from_dn, band, give, take,
+    raw, xc, xs, rhs, yc, ys, acc, from_up, from_dn, band, far, give, take,
     raw_send, raw_recv, up_send, up_recv, dn_send, dn_recv, side_send, side_recv,
 ):
     chunks, _, rows, _ = raw.shape
@@ -302,7 +340,7 @@
     def dn_copy(c, o):
         return remote(acc.at[c, o], from_dn.at[c, o], dn_send.at[c, o], dn_recv.at[c, o], lower)
 
-    for c in range(chunks):
+    def transform(c):
         raws[c].wait_recv()
         mine = pl.ds(pl.multiple_of(odd * rows, rows), rows)
         theirs = pl.ds(pl.multiple_of((1 - odd) * rows, rows), rows)
@@ -320,58 +358,85 @@
         for o in range(groups):
             acc[c, o, :, pl.ds(0, LANES)] = re[o * p_rows : (o + 1) * p_rows]
             acc[c, o, :, pl.ds(LANES, LANES)] = im[o * p_rows : (o + 1) * p_rows]
+
+    def originate(c):
+        @pl.when(z == 0)
+        def _():
+            for o in reversed(range(1, groups)):
+                up_copy(c, o).start()
+
+        @pl.when(z == groups - 1)
+        def _():
+            for o in range(groups - 1):
+                dn_copy(c, o).start()
+
+    def forward(c):
         for k in range(groups):
             far_up, far_dn = (groups - 1 - k, k)
 
-            @pl.when(z < far_up)
+            @pl.when((z > 0) & (z < far_up))
             def _():
-                @pl.when(z > 0)
-                def _():
-                    up_copy(c, far_up).wait_recv()
-                    acc[c, far_up] += from_up[c, far_up]
-
+                up_copy(c, far_up).wait_recv()
+                acc[c, far_up] += from_up[c, far_up]
                 up_copy(c, far_up).start()
 
-            @pl.when(z > far_dn)
+            @pl.when((z < groups - 1) & (z > far_dn))
             def _():
-                @pl.when(z < groups - 1)
-                def _():
-                    dn_copy(c, far_dn).wait_recv()
-                    acc[c, far_dn] += from_dn[c, far_dn]
-
+                dn_copy(c, far_dn).wait_recv()
+                acc[c, far_dn] += from_dn[c, far_dn]
                 dn_copy(c, far_dn).start()
 
-    for c in range(chunks):
+    def collect(g):
         for o in range(groups):
 
             @pl.when(z == o)
             def _():
-                if o > 0:
-                    up_copy(c, o).wait_recv()
-                if o < groups - 1:
-                    dn_copy(c, o).wait_recv()
-                total = acc[c, o]
-                if o > 0:
-                    total = total + from_up[c, o]
-                if o < groups - 1:
-                    total = total + from_dn[c, o]
-                for k, part in enumerate(split(total)):
-                    band[k, pl.ds(0, p_rows), pl.ds(c * LANES, LANES)] = part[:, :LANES]
-                    band[k, pl.ds(p_rows, p_rows), pl.ds(c * LANES, LANES)] = part[:, LANES:]
-
-    left = (band[0], band[1])
-
-    def angles(h):
-        by_cos = dot3(left, (yc[h, 0], yc[h, 1]))
-        by_sin = dot3(left, (ys[h, 0], ys[h, 1]))
+                for i in range(2):
+                    c = 2 * g + i
+                    total = acc[c, o]
+                    if o > 0:
+                        up_copy(c, o).wait_recv()
+                        total = total + from_up[c, o]
+                    if o < groups - 1:
+                        dn_copy(c, o).wait_recv()
+                        total = total + from_dn[c, o]
+                    for k, part in enumerate(split(total)):
+                        band[g, k, pl.ds(0, p_rows), pl.ds(i * LANES, LANES)] = part[:, :LANES]
+                        band[g, k, pl.ds(p_rows, p_rows), pl.ds(i * LANES, LANES)] = part[:, LANES:]
+
+    def angles(g, h):
+        left = (band[g, 0], band[g, 1])
+        y = pl.ds(2 * g * LANES, 2 * LANES)
+        by_cos = dot3(left, (yc[h, 0, y], yc[h, 1, y]))
+        by_sin = dot3(left, (ys[h, 0, y], ys[h, 1, y]))
         return (by_cos[:p_rows] + by_sin[p_rows:], by_cos[p_rows:] - by_sin[:p_rows])
 
-    re, im = angles(1 - iy)
-    give[0] = re
-    give[1] = im
+    final = chunks // 2 - 1
+
+    def accumulate(g):
+        for h in range(2):
+            for d, value in enumerate(angles(g, h)):
+                far[h, d] = value if g == 0 else far[h, d] + value
+
+    for c in range(chunks):
+        transform(c)
+        originate(c)
+        if c > 0:
+            forward(c - 1)
+        if c >= 3 and c % 2 == 1:
+            collect(c // 2 - 1)
+            accumulate(c // 2 - 1)
+    forward(chunks - 1)
+    collect(final)
+
+    def finish(h):
+        pair_of = angles(final, h)
+        return [far[h, d] + pair_of[d] for d in range(2)]
+
+    give[0], give[1] = finish(1 - iy)
     swap = remote(give, take, side_send.at[0], side_recv.at[0], side)
     swap.start()
-    re, im = angles(iy)
+    re, im = finish(iy)
     swap.wait_recv()
     out[0] = re + take[0]
     out[1] = im + take[1]
@@ -439,7 +504,8 @@
             stage,
             stage,
             stage,
-            pltpu.VMEM((2, 2 * p_rows, cols), BF16),
+            pltpu.VMEM((chunks // 2, 2, 2 * p_rows, 2 * LANES), BF16),
+            pltpu.VMEM((2, 2, p_rows, half_q), F32),
             pltpu.VMEM((2, p_rows, half_q), F32),
             pltpu.VMEM((2, p_rows, half_q), F32),
             dma((chunks,)),
@@ -462,8 +528,7 @@
     _, rows, cols = field.shape
     count_x = lax.axis_size("gx")
     angles = tables(rows, cols, count_x, lax.axis_size("gy"))
-    ext_f, ext_l = gather_halo(field, levels)
-    near = propagate(ext_f, ext_l, table)
+    near = propagate(field, levels, gather_halo(field, levels), table)
     return (near, jnp.transpose(far(near, angles, count_x), (1, 0, 2)))
 
 

time: 117 us -> 117 us (level)
  Pallas kernels: 109 us -> 107 us
    pallas_call x1, Pallas kernels: 62.4 us -> 60.7 us  [far(): pl.pallas_call(far_kernel, out_shape=jax.ShapeDtypeStruct((2, p_rows, hal...]
    pallas_call x1, Pallas kernels: 27.6 us -> 28.7 us  [propagate(): pl.pallas_call(functools.partial(heun_kernel, lax.axis_size('gx')), out_s...]
    unnamed x9 -> x17, local copies, waits for them, and re-layouts: 5.67 us -> 6.83 us
where the time goes in v2:
time: 117 us
  Pallas kernels  107 us (91%)
  local copies, waits for them, and re-layouts  6.83 us (6%)
  other arithmetic  2.08 us (2%)
    pallas_call x1, Pallas kernels, far(): pl.pallas_call(far_kernel, out_shape=jax.ShapeDtypeStruct((2, p_rows, hal...  60.7 us
    pallas_call x1, Pallas kernels, propagate(): pl.pallas_call(functools.partial(heun_kernel, lax.axis_size('gx')), out_s...  28.7 us
    pallas_call x1, Pallas kernels, gather_halo(): pl.pallas_call(functools.partial(halo_kernel, lax.axis_size('gx')), out_s...  17.6 us
    unnamed x17, local copies, waits for them, and re-layouts  6.83 us

profile of v2, /device:TPU:0, one launch (start us, length us, event | category | flops | bytes accessed | tf_op | source)
XLA Modules:
  0.0 116.7 jit_solution(8380228698181908122)
XLA Ops:
  0.7 0.0 copy-start
  0.7 1.0 fusion.11
  1.7 0.2 sine_multiply_fusion.1
  1.9 0.0 copy-start.2
  1.9 17.6 %halo.1 = (f32[2,2,32,640]{3,2,1,0:T(8,128)}, s32[2,32,640]{2,1,0:T(8,128)}, f32[2,256,128]{2,1,0:T(8,128)}, s32[256,128]{1,0:T(8,128)}) custom-call(f32[2,256,512]{2,1,0:T(8,128)} %field.3, s32[256,512]{1,0:T(8,128)} %levels.3), custom_call_target="tpu_custom_call" | custom-call | tf_op jit(solution)/shard_map/halo/pallas_call | solution.py:110
  19.5 0.0 copy-start.7
  19.5 0.0 copy-done
  19.5 0.0 copy-done.2
  19.5 0.7 copy-done.7
  20.2 0.0 copy-start.3
  20.2 1.0 copy-done.3
  21.1 0.0 copy-start.4
  21.2 0.9 copy-done.4
  22.1 0.0 copy-start.5
  22.1 0.9 copy-done.5
  23.0 0.0 copy-start.6
  23.0 0.9 copy-done.6
  23.9 28.7 %heun.1.near = f32[2,256,512]{2,1,0:T(8,128)} custom-call(f32[2,256,512]{2,1,0:T(8,128)S(1)} %copy-done, s32[256,512]{1,0:T(8,128)S(1)} %copy-done.2, f32[2,2,32,640]{3,2,1,0:T(8,128)S(1)} %copy-done.3, s32[2,32,640]{2,1,0:T(8,128)S(1)} %copy-done.5, f32[2,256,128]{2,1,0:T(8,128)S(1)} %copy-done.4, s32[256,128]{1,0:T(8,128)S(1)} %copy-done.6, ...), custom_call_target="tpu_custom_call" | custom-call | tf_op jit(solution)/shard_map/heun/pallas_call | solution.py:262
  52.7 0.3 sine_multiply_fusion
  53.0 0.5 fusion.17
  53.5 0.0 copy-start.1
  53.6 1.2 %copy-done.1 = f32[2,256,512]{2,1,0:T(8,128)S(1)} copy-done((f32[2,256,512]{2,1,0:T(8,128)S(1)}, f32[2,256,512]{2,1,0:T(8,128)}, u32[]{:S(2)}) %copy-start.1) | copy-done | bytes 1048600
  54.8 60.7 %far.1 = f32[2,128,512]{2,1,0:T(8,128)S(1)} custom-call(f32[2,256,512]{2,1,0:T(8,128)S(1)} %copy-done.1, f32[4,512]{1,0:T(4,128)S(1)} %get-tuple-element.17.e1c, f32[4,512]{1,0:T(4,128)S(1)} %get-tuple-element.16.e1s, f32[128,512]{1,0:T(8,128)S(1)} %get-tuple-element.19.e2c, f32[128,512]{1,0:T(8,128)S(1)} %get-tuple-element.18.e2s, ...), custom_call_target="tpu_custom_call" | custom-call | tf_op jit(solution)/shard_map/far/pallas_call | solution.py:492
  115.5 1.2 %copy.5 = f32[128,2,512]{2,1,0:T(2,128)} copy(f32[128,2,512]{2,0,1:T(8,128)S(1)} %bitcast.2) | data formatting | bytes 1048576
  (4 shorter events, 0.0 us)
Async XLA Ops:
  0.7 18.9 %copy-start = (f32[2,256,512]{2,1,0:T(8,128)S(1)}, f32[2,256,512]{2,1,0:T(8,128)}, u32[]{:S(2)}) copy-start(f32[2,256,512]{2,1,0:T(8,128)} %field.3) | copy-start | bytes 3145732
  1.9 17.6 %copy-start.2 = (s32[256,512]{1,0:T(8,128)S(1)}, s32[256,512]{1,0:T(8,128)}, u32[]{:S(2)}) copy-start(s32[256,512]{1,0:T(8,128)} %levels.3) | copy-start | bytes 1572868
  19.5 0.7 copy-start.7
  20.2 1.0 copy-start.3
  21.1 0.9 copy-start.4
  22.1 0.9 copy-start.5
  23.0 0.9 copy-start.6
  53.5 1.2 %copy-start.1 = (f32[2,256,512]{2,1,0:T(8,128)S(1)}, f32[2,256,512]{2,1,0:T(8,128)}, u32[]{:S(2)}) copy-start(f32[2,256,512]{2,1,0:T(8,128)} %heun.1.near) | copy-start | bytes 3145732

commit v3 on v2

--- a/solution.py
+++ b/solution.py
@@ -138,7 +138,8 @@
 
 
 def heun_kernel(
-    count_x, field, levels, rows_f, rows_l, side_f, side_l, table, out, buf_f, buf_l, u, mid, con, weight
+    count_x, field, levels, far_rows_f, far_rows_l, far_side_f, far_side_l, table, out,
+    rows_f, rows_l, side_f, side_l, sem, buf_f, buf_l, u, mid, con, weight
 ):
     blocks, tall, _ = buf_l.shape
     deep = tall // 8
@@ -147,19 +148,37 @@
     rows = tall - 2 * HALO
     ix = lax.axis_index("gx")
     iy = lax.axis_index("gy")
+    loads = [
+        pltpu.make_async_copy(far_side_l, side_l, sem.at[0]),
+        pltpu.make_async_copy(far_side_f, side_f, sem.at[1]),
+        pltpu.make_async_copy(far_rows_l, rows_l, sem.at[2]),
+        pltpu.make_async_copy(far_rows_f, rows_f, sem.at[3]),
+    ]
+    for copy in loads:
+        copy.start()
     order = spread_order((wide, wide), blocks, 1)
-    pieces = ((0, HALO), (HALO, rows), (HALO + rows, HALO))
-    for c in range(2):
-        body = jnp.concatenate([field[c], side_f[c]], axis=1)
-        for (start, length), part in zip(pieces, (rows_f[0, c], body, rows_f[1, c])):
-            spread = shuffle(part, order)
-            for j in range(blocks):
-                buf_f[c, j, pl.ds(start, length), :] = spread[:, j * LANES : (j + 1) * LANES]
-    body = jnp.concatenate([levels[...], side_l[...]], axis=1)
-    for (start, length), part in zip(pieces, (rows_l[0], body, rows_l[1])):
+
+    def keep_f(part, c, start, length):
+        spread = shuffle(part, order)
+        for j in range(blocks):
+            buf_f[c, j, pl.ds(start, length), :] = spread[:, j * LANES : (j + 1) * LANES]
+
+    def keep_l(part, start, length):
         spread = jnp.dot(part.astype(F32).astype(BF16), order, preferred_element_type=F32)
         for j in range(blocks):
             buf_l[j, pl.ds(start, length), :] = spread[:, j * LANES : (j + 1) * LANES].astype(jnp.int32)
+
+    loads[0].wait()
+    keep_l(jnp.concatenate([levels[...], side_l[...]], axis=1), HALO, rows)
+    loads[1].wait()
+    for c in range(2):
+        keep_f(jnp.concatenate([field[c], side_f[c]], axis=1), c, HALO, rows)
+    loads[2].wait()
+    loads[3].wait()
+    for end, start in ((0, 0), (1, HALO + rows)):
+        keep_l(rows_l[end], start, HALO)
+        for c in range(2):
+            keep_f(rows_f[end, c], c, start, HALO)
     low = jnp.broadcast_to(table[0:1, :], (8, LANES))
     high = jnp.broadcast_to(table[1:2, :], (8, LANES))
     sub = lax.broadcasted_iota(jnp.int32, (8, LANES), 0)
@@ -255,6 +274,7 @@
     _, rows, cols = field.shape
     tall = rows + 2 * HALO
     blocks = cols // LANES + 1
+    wide = blocks * LANES
     deep = tall // 8
     vmem = pl.BlockSpec(memory_space=pltpu.VMEM)
     state = pltpu.VMEM((2, blocks, deep + 4, 8, LANES), F32)
@@ -262,9 +282,14 @@
     return pl.pallas_call(
         functools.partial(heun_kernel, lax.axis_size("gx")),
         out_shape=jax.ShapeDtypeStruct((2, rows, cols), F32),
-        in_specs=[vmem] * 7,
+        in_specs=[vmem] * 2 + [pl.BlockSpec(memory_space=pl.ANY)] * 4 + [vmem],
         out_specs=vmem,
         scratch_shapes=[
+            pltpu.VMEM((2, 2, HALO, wide), F32),
+            pltpu.VMEM((2, HALO, wide), jnp.int32),
+            pltpu.VMEM((2, rows, LANES), F32),
+            pltpu.VMEM((rows, LANES), jnp.int32),
+            pltpu.SemaphoreType.DMA((4,)),
             pltpu.VMEM((2, blocks, tall, LANES), F32),
             pltpu.VMEM((blocks, tall, LANES), jnp.int32),
             state,

time: 117 us -> 118 us (level)
  no operation moved by 1% of the time
where the time goes in v3:
time: 118 us
  Pallas kernels  108 us (92%)
  local copies, waits for them, and re-layouts  6.83 us (6%)
  other arithmetic  2.08 us (2%)
    pallas_call x1, Pallas kernels, far(): pl.pallas_call(far_kernel, out_shape=jax.ShapeDtypeStruct((2, p_rows, hal...  60.7 us
    pallas_call x1, Pallas kernels, propagate(): pl.pallas_call(functools.partial(heun_kernel, lax.axis_size('gx')), out_s...  29.6 us
    pallas_call x1, Pallas kernels, gather_halo(): pl.pallas_call(functools.partial(halo_kernel, lax.axis_size('gx')), out_s...  17.6 us
    unnamed x17, local copies, waits for them, and re-layouts  6.83 us

profile of v3, /device:TPU:0, one launch (start us, length us, event | category | flops | bytes accessed | tf_op | source)
XLA Modules:
  0.0 117.5 jit_solution(7953650904369492384)
XLA Ops:
  0.7 0.0 copy-start
  0.7 1.0 fusion.11
  1.7 0.2 sine_multiply_fusion.1
  1.9 0.0 copy-start.2
  1.9 17.6 %halo.1 = (f32[2,2,32,640]{3,2,1,0:T(8,128)}, s32[2,32,640]{2,1,0:T(8,128)}, f32[2,256,128]{2,1,0:T(8,128)}, s32[256,128]{1,0:T(8,128)}) custom-call(f32[2,256,512]{2,1,0:T(8,128)} %field.3, s32[256,512]{1,0:T(8,128)} %levels.3), custom_call_target="tpu_custom_call" | custom-call | tf_op jit(solution)/shard_map/halo/pallas_call | solution.py:110
  19.5 0.0 copy-start.7
  19.5 0.0 copy-done
  19.5 0.0 copy-done.2
  19.5 0.7 copy-done.7
  20.2 0.0 copy-start.3
  20.2 1.0 copy-done.3
  21.1 0.0 copy-start.4
  21.2 0.9 copy-done.4
  22.1 0.0 copy-start.5
  22.1 0.9 copy-done.5
  23.0 0.0 copy-start.6
  23.0 0.9 copy-done.6
  23.9 29.6 %heun.1.near = f32[2,256,512]{2,1,0:T(8,128)} custom-call(f32[2,256,512]{2,1,0:T(8,128)S(1)} %copy-done, s32[256,512]{1,0:T(8,128)S(1)} %copy-done.2, f32[2,2,32,640]{3,2,1,0:T(8,128)S(1)} %copy-done.3, s32[2,32,640]{2,1,0:T(8,128)S(1)} %copy-done.5, f32[2,256,128]{2,1,0:T(8,128)S(1)} %copy-done.4, s32[256,128]{1,0:T(8,128)S(1)} %copy-done.6, ...), custom_call_target="tpu_custom_call" | custom-call | tf_op jit(solution)/shard_map/heun/pallas_call | solution.py:282
  53.5 0.3 sine_multiply_fusion
  53.9 0.5 fusion.17
  54.4 0.0 copy-start.1
  54.4 1.2 %copy-done.1 = f32[2,256,512]{2,1,0:T(8,128)S(1)} copy-done((f32[2,256,512]{2,1,0:T(8,128)S(1)}, f32[2,256,512]{2,1,0:T(8,128)}, u32[]{:S(2)}) %copy-start.1) | copy-done | bytes 1048600
  55.6 60.7 %far.1 = f32[2,128,512]{2,1,0:T(8,128)S(1)} custom-call(f32[2,256,512]{2,1,0:T(8,128)S(1)} %copy-done.1, f32[4,512]{1,0:T(4,128)S(1)} %get-tuple-element.17.e1c, f32[4,512]{1,0:T(4,128)S(1)} %get-tuple-element.16.e1s, f32[128,512]{1,0:T(8,128)S(1)} %get-tuple-element.19.e2c, f32[128,512]{1,0:T(8,128)S(1)} %get-tuple-element.18.e2s, ...), custom_call_target="tpu_custom_call" | custom-call | tf_op jit(solution)/shard_map/far/pallas_call | solution.py:517
  116.3 1.2 %copy.5 = f32[128,2,512]{2,1,0:T(2,128)} copy(f32[128,2,512]{2,0,1:T(8,128)S(1)} %bitcast.2) | data formatting | bytes 1048576
  (4 shorter events, 0.0 us)
Async XLA Ops:
  0.7 18.9 %copy-start = (f32[2,256,512]{2,1,0:T(8,128)S(1)}, f32[2,256,512]{2,1,0:T(8,128)}, u32[]{:S(2)}) copy-start(f32[2,256,512]{2,1,0:T(8,128)} %field.3) | copy-start | bytes 3145732
  1.9 17.6 %copy-start.2 = (s32[256,512]{1,0:T(8,128)S(1)}, s32[256,512]{1,0:T(8,128)}, u32[]{:S(2)}) copy-start(s32[256,512]{1,0:T(8,128)} %levels.3) | copy-start | bytes 1572868
  19.5 0.7 copy-start.7
  20.2 1.0 copy-start.3
  21.1 0.9 copy-start.4
  22.1 0.9 copy-start.5
  23.0 0.9 copy-start.6
  54.4 1.2 %copy-start.1 = (f32[2,256,512]{2,1,0:T(8,128)S(1)}, f32[2,256,512]{2,1,0:T(8,128)}, u32[]{:S(2)}) copy-start(f32[2,256,512]{2,1,0:T(8,128)} %heun.1.near) | copy-start | bytes 3145732

commit v4 on v3

--- a/solution.py
+++ b/solution.py
@@ -282,7 +282,7 @@
     return pl.pallas_call(
         functools.partial(heun_kernel, lax.axis_size("gx")),
         out_shape=jax.ShapeDtypeStruct((2, rows, cols), F32),
-        in_specs=[vmem] * 2 + [pl.BlockSpec(memory_space=pl.ANY)] * 4 + [vmem],
+        in_specs=[vmem] * 2 + [pl.BlockSpec(memory_space=pltpu.MemorySpace.HBM)] * 4 + [vmem],
         out_specs=vmem,
         scratch_shapes=[
             pltpu.VMEM((2, 2, HALO, wide), F32),
@@ -297,7 +297,7 @@
             factor,
             factor,
         ],
-        compiler_params=pltpu.CompilerParams(vmem_limit_bytes=40 * 1024 * 1024),
+        compiler_params=pltpu.CompilerParams(vmem_limit_bytes=62 * 1024 * 1024),
         name="heun",
     )(field, levels, *halo, table.reshape(2, LANES))
 

time: 118 us -> 115 us (0.975)
  local copies, waits for them, and re-layouts: 6.83 us -> 2.42 us
    unnamed x17 -> x3, local copies, waits for them, and re-layouts: 6.83 us -> 2.42 us
    pallas_call x1, Pallas kernels: 29.6 us -> 31.3 us  [propagate(): pl.pallas_call(functools.partial(heun_kernel, lax.axis_size('gx')), out_s...]
where the time goes in v4:
time: 115 us
  Pallas kernels  109 us (95%)
  local copies, waits for them, and re-layouts  2.42 us (2%)
  other arithmetic  2.08 us (2%)
    pallas_call x1, Pallas kernels, far(): pl.pallas_call(far_kernel, out_shape=jax.ShapeDtypeStruct((2, p_rows, hal...  60.7 us
    pallas_call x1, Pallas kernels, propagate(): pl.pallas_call(functools.partial(heun_kernel, lax.axis_size('gx')), out_s...  31.3 us
    pallas_call x1, Pallas kernels, gather_halo(): pl.pallas_call(functools.partial(halo_kernel, lax.axis_size('gx')), out_s...  17.6 us
    unnamed x3, local copies, waits for them, and re-layouts  2.42 us

profile of v4, /device:TPU:0, one launch (start us, length us, event | category | flops | bytes accessed | tf_op | source)
XLA Modules:
  0.0 114.7 jit_solution(1160667196181622936)
XLA Ops:
  0.7 1.0 fusion.11
  1.7 0.2 sine_multiply_fusion.1
  1.9 17.6 %halo.1 = (f32[2,2,32,640]{3,2,1,0:T(8,128)}, s32[2,32,640]{2,1,0:T(8,128)}, f32[2,256,128]{2,1,0:T(8,128)}, s32[256,128]{1,0:T(8,128)}) custom-call(f32[2,256,512]{2,1,0:T(8,128)} %field.3, s32[256,512]{1,0:T(8,128)} %levels.3), custom_call_target="tpu_custom_call" | custom-call | tf_op jit(solution)/shard_map/halo/pallas_call | solution.py:110
  19.4 31.3 %heun.1.near = f32[2,256,512]{2,1,0:T(8,128)} custom-call(f32[2,256,512]{2,1,0:T(8,128)} %field.3, s32[256,512]{1,0:T(8,128)} %levels.3, f32[2,2,32,640]{3,2,1,0:T(8,128)} %get-tuple-element.6.far_rows_f, s32[2,32,640]{2,1,0:T(8,128)} %get-tuple-element.7.far_rows_l, f32[2,256,128]{2,1,0:T(8,128)} %get-tuple-element.8.far_side_f, ...), custom_call_target="tpu_custom_call" | custom-call | tf_op jit(solution)/shard_map/heun/pallas_call | solution.py:282
  50.7 0.3 sine_multiply_fusion
  51.1 0.5 fusion.17
  51.6 0.0 copy-start
  51.6 1.2 %copy-done = f32[2,256,512]{2,1,0:T(8,128)S(1)} copy-done((f32[2,256,512]{2,1,0:T(8,128)S(1)}, f32[2,256,512]{2,1,0:T(8,128)}, u32[]{:S(2)}) %copy-start) | copy-done | bytes 1048600
  52.8 60.7 %far.1 = f32[2,128,512]{2,1,0:T(8,128)S(1)} custom-call(f32[2,256,512]{2,1,0:T(8,128)S(1)} %copy-done, f32[4,512]{1,0:T(4,128)S(1)} %get-tuple-element.17.e1c, f32[4,512]{1,0:T(4,128)S(1)} %get-tuple-element.16.e1s, f32[128,512]{1,0:T(8,128)S(1)} %get-tuple-element.19.e2c, f32[128,512]{1,0:T(8,128)S(1)} %get-tuple-element.18.e2s, ...), custom_call_target="tpu_custom_call" | custom-call | tf_op jit(solution)/shard_map/far/pallas_call | solution.py:517
  113.5 1.2 %copy.5 = f32[128,2,512]{2,1,0:T(2,128)} copy(f32[128,2,512]{2,0,1:T(8,128)S(1)} %bitcast.2) | data formatting | bytes 1048576
  (4 shorter events, 0.0 us)
Async XLA Ops:
  51.6 1.2 %copy-start = (f32[2,256,512]{2,1,0:T(8,128)S(1)}, f32[2,256,512]{2,1,0:T(8,128)}, u32[]{:S(2)}) copy-start(f32[2,256,512]{2,1,0:T(8,128)} %heun.1.near) | copy-start | bytes 3145732
